TPU v7x, 256 devices: a whole 4x4x8 slice. The times are simulated.
256 devices in a mesh: seq: 16 (over z_lo, y), head: 16 (over x, z_hi, core).
Axes of the slice: x: 4, y: 4, z: 8 (z_hi: 2, z_lo: 4; z = z_hi * 4 + z_lo), core: 2. Of those that a mesh axis runs over, the one named last changes fastest.
Arguments:
- query: bfloat16 [16384, 2048], P(('seq', 'head')), may hold values from -6 to 6
- key: bfloat16 [16384, 2048], P(('seq', 'head')), may hold values from -6 to 6
- value: bfloat16 [16384, 2048], P(('seq', 'head')), may hold values from -6 to 6
- output: bfloat16 [16384, 2048], P(('seq', 'head')), may hold values from -6 to 6
- grad_out: bfloat16 [16384, 2048], P(('seq', 'head')), may hold values from -6 to 6
- logsumexp: float32 [16, 16384], P('head', 'seq'), may hold values from 3.5 to 8.5, as said below
- rand_blocks: int32 [256, 3], replicated, may hold values from 0 to 255, as said below
Outputs:
- grad_query: bfloat16 [16384, 2048], P(('seq', 'head'))
- grad_key: bfloat16 [16384, 2048], P(('seq', 'head'))
- grad_value: bfloat16 [16384, 2048], P(('seq', 'head'))
Inputs may be any that keep to these rules, and one draw needn't show every extreme that they name: `rand_blocks`: each row names 3 different blocks, none below 2 and none within one block of the row's own block. In aligned runs of 16 rows, exactly 3 of the run's entries fall in each aligned run of 16 key blocks. `logsumexp`: rows of the first 2 blocks lie between 7 and 8.5, all others between 3.5 and 5.
All inputs are finite; a program needn't handle non-finite values.
Results may differ from a plain program's by a relative error of at most 0.02.
Values may be sent and summed in bfloat16 or wider, within the bound.
No kernel may reach another device: no remote copies, remote signals or barrier semaphores. Data moves between devices by JAX's collectives and lax.ppermute only.
A program may use at most 64 MiB of HBM per device.

v0:
```python
import jax
import jax.numpy as jnp
from jax import lax
from jax.sharding import PartitionSpec as P

HEADS = 16
HD = 128
BLK = 64
GLOB = 2
RAND = 3


def spread(value, axis, source):
    kept = jnp.where(lax.axis_index(axis) == source, value, 0).astype(value.dtype)
    return lax.psum(kept, axis)


def passed_along(value, axis, steps):
    count = lax.axis_size(axis)
    initial, last = (max(0, -steps), min(count, count - steps))
    return lax.ppermute(value, axis, [(source, source + steps) for source in range(initial, last)])


def block_grads(queries, grad_rows, log_norm, deltas, keys, values, usable, factor):
    scores = (
        jnp.einsum("...md,...nd->...mn", queries, keys, preferred_element_type=jnp.float32) * factor
    )
    weights = jnp.where(usable, jnp.exp(scores - log_norm[..., None]), 0.0)
    weights_low = weights.astype(jnp.bfloat16)
    grad_values = jnp.einsum(
        "...mn,...md->...nd", weights_low, grad_rows, preferred_element_type=jnp.float32
    )
    grad_probs = jnp.einsum(
        "...md,...nd->...mn", grad_rows, values, preferred_element_type=jnp.float32
    )
    grad_scores = (weights * (grad_probs - deltas[..., None])).astype(jnp.bfloat16)
    grad_queries = (
        jnp.einsum("...mn,...nd->...md", grad_scores, keys, preferred_element_type=jnp.float32)
        * factor
    )
    grad_keys = (
        jnp.einsum("...mn,...md->...nd", grad_scores, queries, preferred_element_type=jnp.float32)
        * factor
    )
    return (grad_queries, grad_keys, grad_values)


def slide_blocks(stack, offset):
    if offset == 0:
        return stack
    blank = jnp.zeros_like(stack[:, :1])
    if offset > 0:
        return jnp.concatenate([stack[:, 1:], blank], axis=1)
    return jnp.concatenate([blank, stack[:, :-1]], axis=1)


def slot_order(rand_blocks, group_id, blocks_here):
    pattern_rows = lax.dynamic_slice_in_dim(rand_blocks, group_id * blocks_here, blocks_here, 0)
    entries = pattern_rows.reshape(-1)
    ranking = jnp.argsort(entries // blocks_here, stable=True)
    slot_query = ranking // rand_blocks.shape[1]
    slot_key = entries[ranking] % blocks_here
    return (slot_query, slot_key)


def per_device(query, key, value, output, grad_out, logsumexp, rand_blocks):
    tok_rows = query.shape[0]
    heads_here = logsumexp.shape[0]
    seq_rows = logsumexp.shape[1]
    blocks_here = seq_rows // BLK
    groups = lax.axis_size("seq")
    position = lax.axis_index("seq")
    per_group = RAND * blocks_here // groups
    glob_rows = GLOB * BLK
    factor = HD ** (-0.5)

    def to_heads(matrix):
        return matrix.reshape(tok_rows, HEADS, HD).transpose(1, 0, 2)

    query_rows, key_rows, value_rows, out_rows, grad_rows = (
        lax.all_to_all(to_heads(query), "head", split_axis=0, concat_axis=1, tiled=True),
        lax.all_to_all(to_heads(key), "head", split_axis=0, concat_axis=1, tiled=True),
        lax.all_to_all(to_heads(value), "head", split_axis=0, concat_axis=1, tiled=True),
        lax.all_to_all(to_heads(output), "head", split_axis=0, concat_axis=1, tiled=True),
        lax.all_to_all(to_heads(grad_out), "head", split_axis=0, concat_axis=1, tiled=True),
    )
    deltas = jnp.sum(grad_rows.astype(jnp.float32) * out_rows.astype(jnp.float32), axis=-1)

    def as_blocks(stack):
        return stack.reshape((heads_here, blocks_here, BLK) + stack.shape[2:])

    query_blk = as_blocks(query_rows)
    key_blk = as_blocks(key_rows)
    value_blk = as_blocks(value_rows)
    grad_blk = as_blocks(grad_rows)
    norm_blk = as_blocks(logsumexp)
    delta_blk = as_blocks(deltas)
    block_ids = jnp.arange(blocks_here, dtype=jnp.int32)
    first_id = position * blocks_here
    query_alive = first_id + block_ids >= GLOB
    grad_query = jnp.zeros((heads_here, blocks_here, BLK, HD), jnp.float32)
    grad_key_home = jnp.zeros_like(grad_query)
    grad_value_home = jnp.zeros_like(grad_query)
    for offset in (-1, 0, 1):
        target = block_ids + offset
        usable = query_alive & (target >= 0) & (target < blocks_here) & (first_id + target >= GLOB)
        part_q, part_k, part_v = block_grads(
            query_blk,
            grad_blk,
            norm_blk,
            delta_blk,
            slide_blocks(key_blk, offset),
            slide_blocks(value_blk, offset),
            usable[None, :, None, None],
            factor,
        )
        grad_query = grad_query + part_q
        grad_key_home = grad_key_home + slide_blocks(part_k, -offset)
        grad_value_home = grad_value_home + slide_blocks(part_v, -offset)
    row_alive = jnp.repeat(query_alive, BLK)
    at_home = (position == 0).astype(jnp.float32)
    glob_key, glob_value, glob_query, glob_grad = (
        spread(key_rows[:, :glob_rows], "seq", 0),
        spread(value_rows[:, :glob_rows], "seq", 0),
        spread(query_rows[:, :glob_rows], "seq", 0),
        spread(grad_rows[:, :glob_rows], "seq", 0),
    )
    glob_norm, glob_delta = (
        spread(logsumexp[:, :glob_rows], "seq", 0),
        spread(deltas[:, :glob_rows], "seq", 0),
    )
    key_part_q, key_part_k, key_part_v = block_grads(
        query_rows,
        grad_rows,
        logsumexp,
        deltas,
        glob_key,
        glob_value,
        row_alive[None, :, None],
        factor,
    )
    grad_query = grad_query + as_blocks(key_part_q)
    spread_q, spread_k, spread_v = block_grads(
        glob_query, glob_grad, glob_norm, glob_delta, key_rows, value_rows, True, factor
    )
    grad_key_home = grad_key_home + as_blocks(spread_k)
    grad_value_home = grad_value_home + as_blocks(spread_v)
    totals_k, totals_v, totals_q = (
        lax.psum(key_part_k.astype(jnp.bfloat16), "seq").astype(jnp.float32),
        lax.psum(key_part_v.astype(jnp.bfloat16), "seq").astype(jnp.float32),
        lax.psum(spread_q.astype(jnp.bfloat16), "seq").astype(jnp.float32),
    )
    grad_query = grad_query.at[:, :GLOB].add(at_home * totals_q.reshape(heads_here, GLOB, BLK, HD))
    grad_key_home = grad_key_home.at[:, :GLOB].add(
        at_home * totals_k.reshape(heads_here, GLOB, BLK, HD)
    )
    grad_value_home = grad_value_home.at[:, :GLOB].add(
        at_home * totals_v.reshape(heads_here, GLOB, BLK, HD)
    )
    slot_q = slot_order(rand_blocks, position, blocks_here)[0]

    def wanted(anchor):
        return slot_order(rand_blocks, anchor, blocks_here)[1]

    all_wanted = jax.vmap(wanted)(jnp.arange(groups, dtype=jnp.int32))
    send_ids = lax.dynamic_slice_in_dim(all_wanted, position * per_group, per_group, 1).reshape(-1)
    far_key, far_value = (
        lax.all_to_all(key_blk[:, send_ids], "seq", split_axis=1, concat_axis=1, tiled=True),
        lax.all_to_all(value_blk[:, send_ids], "seq", split_axis=1, concat_axis=1, tiled=True),
    )
    usable = first_id + slot_q >= GLOB
    part_q, part_k, part_v = block_grads(
        query_blk[:, slot_q],
        grad_blk[:, slot_q],
        norm_blk[:, slot_q],
        delta_blk[:, slot_q],
        far_key,
        far_value,
        usable[None, :, None, None],
        factor,
    )
    grad_query = grad_query.at[:, slot_q].add(part_q)
    back_key, back_value = (
        lax.all_to_all(part_k, "seq", split_axis=1, concat_axis=1, tiled=True),
        lax.all_to_all(part_v, "seq", split_axis=1, concat_axis=1, tiled=True),
    )
    grad_key_home = grad_key_home.at[:, send_ids].add(back_key)
    grad_value_home = grad_value_home.at[:, send_ids].add(back_value)
    left_key, left_value = passed_along((key_blk[:, -1:], value_blk[:, -1:]), "seq", 1)
    right_key, right_value = passed_along((key_blk[:, :1], value_blk[:, :1]), "seq", -1)
    left_ok = (position >= 1) & (first_id - 1 >= GLOB)
    right_ok = (position <= groups - 2) & (first_id + blocks_here - 1 >= GLOB)
    left_q, left_k, left_v = block_grads(
        query_blk[:, :1],
        grad_blk[:, :1],
        norm_blk[:, :1],
        delta_blk[:, :1],
        left_key,
        left_value,
        left_ok,
        factor,
    )
    right_q, right_k, right_v = block_grads(
        query_blk[:, -1:],
        grad_blk[:, -1:],
        norm_blk[:, -1:],
        delta_blk[:, -1:],
        right_key,
        right_value,
        right_ok,
        factor,
    )
    grad_query = grad_query.at[:, :1].add(left_q)
    grad_query = grad_query.at[:, -1:].add(right_q)
    from_right_k, from_right_v = (
        passed_along(left_k.astype(jnp.bfloat16), "seq", -1).astype(left_k.dtype),
        passed_along(left_v.astype(jnp.bfloat16), "seq", -1).astype(left_v.dtype),
    )
    from_left_k, from_left_v = (
        passed_along(right_k.astype(jnp.bfloat16), "seq", 1).astype(right_k.dtype),
        passed_along(right_v.astype(jnp.bfloat16), "seq", 1).astype(right_v.dtype),
    )
    grad_key_home = grad_key_home.at[:, -1:].add(from_right_k)
    grad_value_home = grad_value_home.at[:, -1:].add(from_right_v)
    grad_key_home = grad_key_home.at[:, :1].add(from_left_k)
    grad_value_home = grad_value_home.at[:, :1].add(from_left_v)

    def to_rows(stack):
        return stack.astype(jnp.bfloat16).reshape(heads_here, seq_rows, HD)

    back_q, back_k, back_v = (
        lax.all_to_all(to_rows(grad_query), "head", split_axis=1, concat_axis=0, tiled=True),
        lax.all_to_all(to_rows(grad_key_home), "head", split_axis=1, concat_axis=0, tiled=True),
        lax.all_to_all(to_rows(grad_value_home), "head", split_axis=1, concat_axis=0, tiled=True),
    )

    def to_tokens(stack):
        return stack.transpose(1, 0, 2).reshape(tok_rows, HEADS * HD)

    return (to_tokens(back_q), to_tokens(back_k), to_tokens(back_v))


def solution(mesh):
    in_specs = (
        P(("seq", "head"), None),
        P(("seq", "head"), None),
        P(("seq", "head"), None),
        P(("seq", "head"), None),
        P(("seq", "head"), None),
        P("head", "seq"),
        P(),
    )
    out_specs = (P(("seq", "head"), None), P(("seq", "head"), None), P(("seq", "head"), None))
    return jax.shard_map(
        per_device, mesh=mesh, in_specs=in_specs, out_specs=out_specs, check_vma=False
    )
```

profile of v0, /device:TPU:64, one launch (start us, length us, event | category | flops | bytes accessed | tf_op | source)
XLA Modules:
  0.0 658.4 jit_solution(3117383005306899725)
XLA Ops:
  8.9 9.2 %all-to-all-start = ((bf16[16,64,128]{2,1,0:T(8,128)(2,1)}), bf16[16,64,128]{2,1,0:T(8,128)(2,1)S(1)}, u32[]{:S(2)}, u32[]{:S(2)}) async-start(bf16[16,64,128]{2,1,0:T(8,128)(2,1)} %bitcast_bitcast_fusion.4), calls=%async_computation | async-start | bytes 524288 | tf_op jit(solution)/shard_map/all_to_all | solution.py:82
  18.2 32.0 %while.10 = (s32[]{:T(128)}, s32[256,3]{0,1:T(4,128)}, s32[16,2]{0,1:T(2,128)S(1)}, s32[16,16,3]{1,2,0:T(4,128)S(1)}, s32[]{:T(128)}) while((s32[]{:T(128)}, s32[256,3]{0,1:T(4,128)}, s32[16,2]{0,1:T(2,128)S(1)}, s32[16,16,3]{1,2,0:T(4,128)S(1)}, s32[]{:T(128)}) %tuple.65), condition=%wide.while_cond.9, body=%wide.while_body.9.sunk | while | flops 2 | bytes 2345 | solution.py:58
  51.5 5.3 gather_fusion.6
  61.6 9.6 %all-to-all-start.2 = ((bf16[16,64,128]{2,1,0:T(8,128)(2,1)}), bf16[16,64,128]{2,1,0:T(8,128)(2,1)S(1)}, u32[]{:S(2)}, u32[]{:S(2)}) async-start(bf16[16,64,128]{2,1,0:T(8,128)(2,1)} %bitcast_bitcast_fusion.2), calls=%async_computation.2 | async-start | bytes 524288 | tf_op jit(solution)/shard_map/all_to_all | solution.py:83
  72.1 13.9 %all-to-all-done.2 = bf16[16,64,128]{2,1,0:T(8,128)(2,1)S(1)} async-done(((bf16[16,64,128]{2,1,0:T(8,128)(2,1)}), bf16[16,64,128]{2,1,0:T(8,128)(2,1)S(1)}, u32[]{:S(2)}, u32[]{:S(2)}) %all-to-all-start.2) | async-done | bytes 262176 | tf_op jit(solution)/shard_map/all_to_all | solution.py:83
  86.0 3.5 all-to-all-start.4
  91.6 10.8 %all-to-all-done.4 = bf16[16,64,128]{2,1,0:T(8,128)(2,1)S(1)} async-done(((bf16[16,64,128]{2,1,0:T(8,128)(2,1)}), bf16[16,64,128]{2,1,0:T(8,128)(2,1)S(1)}, u32[]{:S(2)}, u32[]{:S(2)}) %all-to-all-start.4) | async-done | bytes 262176 | tf_op jit(solution)/shard_map/all_to_all | solution.py:84
  102.4 3.5 all-to-all-start.3
  109.1 8.8 %all-to-all-done.3 = bf16[16,64,128]{2,1,0:T(8,128)(2,1)S(1)} async-done(((bf16[16,64,128]{2,1,0:T(8,128)(2,1)}), bf16[16,64,128]{2,1,0:T(8,128)(2,1)S(1)}, u32[]{:S(2)}, u32[]{:S(2)}) %all-to-all-start.3) | async-done | bytes 262176 | tf_op jit(solution)/shard_map/all_to_all | solution.py:85
  118.0 3.5 all-to-all-start.1
  124.0 9.5 %all-to-all-done.1 = bf16[16,64,128]{2,1,0:T(8,128)(2,1)S(1)} async-done(((bf16[16,64,128]{2,1,0:T(8,128)(2,1)}), bf16[16,64,128]{2,1,0:T(8,128)(2,1)S(1)}, u32[]{:S(2)}, u32[]{:S(2)}) %all-to-all-start.1) | async-done | bytes 262176 | tf_op jit(solution)/shard_map/all_to_all | solution.py:81
  134.7 5.4 collective-permute-start.2
  142.6 6.0 collective-permute-start.3
  155.6 7.3 %all-to-all-start.5 = ((bf16[1,48,64,128]{3,2,0,1:T(8,128)(2,1)}), bf16[1,48,64,128]{3,2,0,1:T(8,128)(2,1)S(1)}, u32[]{:S(2)}, u32[]{:S(2)}) async-start(bf16[1,48,64,128]{3,2,0,1:T(8,128)(2,1)} %bitcast.32), calls=%async_computation.5 | async-start | bytes 1572864 | tf_op jit(solution)/shard_map/all_to_all | solution.py:168
  170.5 36.8 %all-reduce.9 = (f32[128]{0:T(128)}, f32[128]{0:T(128)S(1)}) all-reduce(f32[128]{0:T(128)S(1)} %copy-done.53, f32[128]{0:T(128)S(1)} %copy-done.54), channel_id=1, replica_groups=mesh['seq'=16,'head'=16] {'seq'}, use_global_device_ids=true, to_apply=%region_4.5 | all-reduce | flops 256 | bytes 2048 | tf_op jit(solution)/shard_map/psum | solution.py:15
  207.8 107.8 %all-reduce.17.cloned.1.call-done = (bf16[128,128]{1,0:T(8,128)(2,1)}, bf16[128,128]{1,0:T(8,128)(2,1)}, bf16[128,128]{1,0:T(8,128)(2,1)}, bf16[128,128]{1,0:T(8,128)(2,1)}) async-done(((bf16[128,128]{1,0:T(8,128)(2,1)}, bf16[128,128]{1,0:T(8,128)(2,1)}, bf16[128,128]{1,0:T(8,128)(2,1)}, bf16[128,128]{1,0:T(8,128)(2,1)}), (bf16[128,128]{1,0:T(8,128)(2,1)}, bf16[128,128]{1,0:T(8,128)(2,1)}, ...) | async-done | bytes 131088 | tf_op jit(solution)/shard_map/psum | solution.py:15
  320.6 14.9 %all-to-all-start.6 = ((bf16[1,48,64,128]{3,2,0,1:T(8,128)(2,1)}), bf16[1,48,64,128]{3,2,0,1:T(8,128)(2,1)}, u32[]{:S(2)}, u32[]{:S(2)}) async-start(bf16[1,48,64,128]{3,2,0,1:T(8,128)(2,1)} %bitcast.35), calls=%async_computation.6 | async-start | bytes 1572864 | tf_op jit(solution)/shard_map/all_to_all | solution.py:169
  340.1 144.8 %all-reduce.15.cloned.1.call-done = (bf16[1,128,128]{2,1,0:T(8,128)(2,1)}, bf16[1,128,128]{2,1,0:T(8,128)(2,1)}, bf16[1,128,128]{2,1,0:T(8,128)(2,1)}) async-done(((bf16[1,128,128]{2,1,0:T(8,128)(2,1)}, bf16[1,128,128]{2,1,0:T(8,128)(2,1)}, bf16[1,128,128]{2,1,0:T(8,128)(2,1)}), (bf16[1,128,128]{2,1,0:T(8,128)(2,1)}, bf16[1,128,128]{2,1,0:T(8,128)(2,1)}, ...) | async-done | bytes 98320 | tf_op jit(solution)/shard_map/psum | solution.py:151
  492.5 5.4 scatter_fusion
  502.0 8.2 %all-to-all-start.7 = ((bf16[16,2,4096]{2,1,0:T(2,128)(2,1)}), bf16[16,2,4096]{2,1,0:T(2,128)(2,1)S(1)}, u32[]{:S(2)}, u32[]{:S(2)}) async-start(bf16[16,2,4096]{2,1,0:T(2,128)(2,1)} %reshape.1100), calls=%async_computation.7 | async-start | bytes 524288 | tf_op jit(solution)/shard_map/all_to_all | solution.py:232
  513.3 9.0 %all-to-all-done.7 = bf16[16,2,4096]{2,1,0:T(2,128)(2,1)S(1)} async-done(((bf16[16,2,4096]{2,1,0:T(2,128)(2,1)}), bf16[16,2,4096]{2,1,0:T(2,128)(2,1)S(1)}, u32[]{:S(2)}, u32[]{:S(2)}) %all-to-all-start.7) | async-done | bytes 262176 | tf_op jit(solution)/shard_map/all_to_all | solution.py:232
  522.3 11.6 %all-to-all-start.10 = ((f32[1,48,64,128]{3,2,0,1:T(8,128)}), f32[1,48,64,128]{3,2,0,1:T(8,128)}, u32[]{:S(2)}, u32[]{:S(2)}) async-start(f32[1,48,64,128]{3,2,0,1:T(8,128)} %convolution_bitcast_fusion), calls=%async_computation.10 | async-start | bytes 3145728 | tf_op jit(solution)/shard_map/all_to_all | solution.py:185
  535.5 35.5 %all-to-all-done.10 = f32[1,48,64,128]{3,2,0,1:T(8,128)} async-done(((f32[1,48,64,128]{3,2,0,1:T(8,128)}), f32[1,48,64,128]{3,2,0,1:T(8,128)}, u32[]{:S(2)}, u32[]{:S(2)}) %all-to-all-start.10) | async-done | bytes 1572896 | tf_op jit(solution)/shard_map/all_to_all | solution.py:185
  571.0 5.1 all-to-all-start.8
  578.9 3.5 collective-permute-start.5
  582.6 4.6 collective-permute-start.4
  600.6 5.4 scatter_fusion.2
  606.0 3.5 collective-permute-done.6
  616.8 4.2 all-to-all-start.11
  628.9 4.0 all-to-all-done.11
  632.9 5.6 all-to-all-start.9
  640.7 9.8 %all-to-all-done.9 = bf16[16,2,4096]{2,1,0:T(2,128)(2,1)S(1)} async-done(((bf16[16,2,4096]{2,1,0:T(2,128)(2,1)}), bf16[16,2,4096]{2,1,0:T(2,128)(2,1)S(1)}, u32[]{:S(2)}, u32[]{:S(2)}) %all-to-all-start.9) | async-done | bytes 262176 | tf_op jit(solution)/shard_map/all_to_all | solution.py:233
  (325 shorter events, 127.0 us)
Async XLA Ops:
  8.9 52.7 %all-to-all-start = ((bf16[16,64,128]{2,1,0:T(8,128)(2,1)}), bf16[16,64,128]{2,1,0:T(8,128)(2,1)S(1)}, u32[]{:S(2)}, u32[]{:S(2)}) async-start(bf16[16,64,128]{2,1,0:T(8,128)(2,1)} %bitcast_bitcast_fusion.4), calls=%async_computation | async-start | bytes 524288 | tf_op jit(solution)/shard_map/all_to_all | solution.py:82
  56.8 33.2 %copy-start.29 = (bf16[64,2048]{1,0:T(8,128)(2,1)S(1)}, bf16[64,2048]{1,0:T(8,128)(2,1)}, u32[]{:S(2)}) copy-start(bf16[64,2048]{1,0:T(8,128)(2,1)} %param.25) | copy-start | bytes 786436
  56.9 34.0 %copy-start.30 = (bf16[64,2048]{1,0:T(8,128)(2,1)S(1)}, bf16[64,2048]{1,0:T(8,128)(2,1)}, u32[]{:S(2)}) copy-start(bf16[64,2048]{1,0:T(8,128)(2,1)} %param.29) | copy-start | bytes 786436
  61.6 24.4 %all-to-all-start.2 = ((bf16[16,64,128]{2,1,0:T(8,128)(2,1)}), bf16[16,64,128]{2,1,0:T(8,128)(2,1)S(1)}, u32[]{:S(2)}, u32[]{:S(2)}) async-start(bf16[16,64,128]{2,1,0:T(8,128)(2,1)} %bitcast_bitcast_fusion.2), calls=%async_computation.2 | async-start | bytes 524288 | tf_op jit(solution)/shard_map/all_to_all | solution.py:83
  86.0 16.4 %all-to-all-start.4 = ((bf16[16,64,128]{2,1,0:T(8,128)(2,1)}), bf16[16,64,128]{2,1,0:T(8,128)(2,1)S(1)}, u32[]{:S(2)}, u32[]{:S(2)}) async-start(bf16[16,64,128]{2,1,0:T(8,128)(2,1)} %bitcast_bitcast_fusion), calls=%async_computation.4 | async-start | bytes 524288 | tf_op jit(solution)/shard_map/all_to_all | solution.py:84
  102.4 15.6 %all-to-all-start.3 = ((bf16[16,64,128]{2,1,0:T(8,128)(2,1)}), bf16[16,64,128]{2,1,0:T(8,128)(2,1)S(1)}, u32[]{:S(2)}, u32[]{:S(2)}) async-start(bf16[16,64,128]{2,1,0:T(8,128)(2,1)} %bitcast_bitcast_fusion.1), calls=%async_computation.3 | async-start | bytes 524288 | tf_op jit(solution)/shard_map/all_to_all | solution.py:85
  118.0 15.5 %all-to-all-start.1 = ((bf16[16,64,128]{2,1,0:T(8,128)(2,1)}), bf16[16,64,128]{2,1,0:T(8,128)(2,1)S(1)}, u32[]{:S(2)}, u32[]{:S(2)}) async-start(bf16[16,64,128]{2,1,0:T(8,128)(2,1)} %bitcast_bitcast_fusion.3), calls=%async_computation.1 | async-start | bytes 524288 | tf_op jit(solution)/shard_map/all_to_all | solution.py:81
  134.7 72.6 %collective-permute-start.2 = (bf16[1,1,64,128]{3,2,1,0:T(8,128)(2,1)S(1)}, bf16[1,1,64,128]{3,2,1,0:T(8,128)(2,1)S(1)}, u32[]{:S(2)}, u32[]{:S(2)}) collective-permute-start(bf16[1,1,64,128]{3,2,1,0:T(8,128)(2,1)S(1)} %get-tuple-element.144), channel_id=1, source_target_pairs={{16,0},{32,16},{48,32},{64,48},{80,64},{96,80},{112,96},{128,112},... | collective-permute-start | bytes 49160 | tf_op jit(solution)/shard_map/ppermute | solution.py:21
  140.1 67.4 %collective-permute-start = (bf16[1,1,64,128]{3,2,1,0:T(8,128)(2,1)S(1)}, bf16[1,1,64,128]{3,2,1,0:T(8,128)(2,1)S(1)}, u32[]{:S(2)}, u32[]{:S(2)}) collective-permute-start(bf16[1,1,64,128]{3,2,1,0:T(8,128)(2,1)S(1)} %get-tuple-element.145), channel_id=1, source_target_pairs={{0,16},{16,32},{32,48},{48,64},{64,80},{80,96},{96,112},{112,128},... | collective-permute-start | bytes 49160 | tf_op jit(solution)/shard_map/ppermute | solution.py:21
  142.6 64.8 %collective-permute-start.3 = (bf16[1,1,64,128]{3,2,1,0:T(8,128)(2,1)S(1)}, bf16[1,1,64,128]{3,2,1,0:T(8,128)(2,1)S(1)}, u32[]{:S(2)}, u32[]{:S(2)}) collective-permute-start(bf16[1,1,64,128]{3,2,1,0:T(8,128)(2,1)S(1)} %get-tuple-element.142), channel_id=1, source_target_pairs={{16,0},{32,16},{48,32},{64,48},{80,64},{96,80},{112,96},{128,112},... | collective-permute-start | bytes 49160 | tf_op jit(solution)/shard_map/ppermute | solution.py:21
  148.7 59.1 %collective-permute-start.1 = (bf16[1,1,64,128]{3,2,1,0:T(8,128)(2,1)S(1)}, bf16[1,1,64,128]{3,2,1,0:T(8,128)(2,1)S(1)}, u32[]{:S(2)}, u32[]{:S(2)}) collective-permute-start(bf16[1,1,64,128]{3,2,1,0:T(8,128)(2,1)S(1)} %get-tuple-element.143), channel_id=1, source_target_pairs={{0,16},{16,32},{32,48},{48,64},{64,80},{80,96},{96,112},{112,128},... | collective-permute-start | bytes 49160 | tf_op jit(solution)/shard_map/ppermute | solution.py:21
  155.6 165.0 %all-to-all-start.5 = ((bf16[1,48,64,128]{3,2,0,1:T(8,128)(2,1)}), bf16[1,48,64,128]{3,2,0,1:T(8,128)(2,1)S(1)}, u32[]{:S(2)}, u32[]{:S(2)}) async-start(bf16[1,48,64,128]{3,2,0,1:T(8,128)(2,1)} %bitcast.32), calls=%async_computation.5 | async-start | bytes 1572864 | tf_op jit(solution)/shard_map/all_to_all | solution.py:168
  163.0 152.7 %all-reduce.17.cloned.1.call-start = ((), (), s32[]{:S(2)}) async-start(), calls=%async_computation.13 | async-start | bytes 262144 | tf_op jit(solution)/shard_map/psum | solution.py:15
  168.9 146.7 %copy-start.48 = (pred[1024]{0:T(1024)(128)(4,1)S(1)}, pred[1024]{0:T(1024)(128)(4,1)}, u32[]{:S(2)}) copy-start(pred[1024]{0:T(1024)(128)(4,1)} %broadcast_in_dim.110) | copy-start | bytes 3076
  207.4 108.2 %copy-start.34 = (f32[64,64]{1,0:T(8,128)}, f32[64,64]{1,0:T(8,128)S(1)}, u32[]{:S(2)}) copy-start(f32[64,64]{1,0:T(8,128)S(1)} %fusion.41) | copy-start | bytes 49156
  207.5 111.3 %copy-start.44 = (bf16[1,1,64,128]{3,2,1,0:T(8,128)(2,1)}, bf16[1,1,64,128]{3,2,1,0:T(8,128)(2,1)S(1)}, u32[]{:S(2)}) copy-start(bf16[1,1,64,128]{3,2,1,0:T(8,128)(2,1)S(1)} %collective-permute-done) | copy-start | bytes 49156
  207.7 107.9 %copy-start.36 = (f32[64,64]{1,0:T(8,128)}, f32[64,64]{1,0:T(8,128)S(1)}, u32[]{:S(2)}) copy-start(f32[64,64]{1,0:T(8,128)S(1)} %fusion.46) | copy-start | bytes 49156
  320.6 168.0 %all-to-all-start.6 = ((bf16[1,48,64,128]{3,2,0,1:T(8,128)(2,1)}), bf16[1,48,64,128]{3,2,0,1:T(8,128)(2,1)}, u32[]{:S(2)}, u32[]{:S(2)}) async-start(bf16[1,48,64,128]{3,2,0,1:T(8,128)(2,1)} %bitcast.35), calls=%async_computation.6 | async-start | bytes 1572864 | tf_op jit(solution)/shard_map/all_to_all | solution.py:169
  335.5 149.4 %all-reduce.15.cloned.1.call-start = ((), (), s32[]{:S(2)}) async-start(), calls=%async_computation.12 | async-start | bytes 196608 | tf_op jit(solution)/shard_map/psum | solution.py:151
  337.4 148.3 %copy-start.3 = (bf16[48,64,128]{2,1,0:T(8,128)(2,1)S(1)}, bf16[48,64,128]{2,1,0:T(8,128)(2,1)}, u32[]{:S(2)}) copy-start(bf16[48,64,128]{2,1,0:T(8,128)(2,1)} %gather_fusion) | copy-start | bytes 2359300
  337.5 148.3 %copy-start.51 = (pred[48]{0:T(512)(128)(4,1)S(1)}, pred[48]{0:T(512)(128)(4,1)}, u32[]{:S(2)}) copy-start(pred[48]{0:T(512)(128)(4,1)} %get-tuple-element.140) | copy-start | bytes 148
  338.7 147.0 %copy-start.43 = (f32[48,64]{1,0:T(8,128)S(1)}, f32[48,64]{1,0:T(8,128)}, u32[]{:S(2)}) copy-start(f32[48,64]{1,0:T(8,128)} %gather_fusion.2) | copy-start | bytes 36868
  502.0 20.3 %all-to-all-start.7 = ((bf16[16,2,4096]{2,1,0:T(2,128)(2,1)}), bf16[16,2,4096]{2,1,0:T(2,128)(2,1)S(1)}, u32[]{:S(2)}, u32[]{:S(2)}) async-start(bf16[16,2,4096]{2,1,0:T(2,128)(2,1)} %reshape.1100), calls=%async_computation.7 | async-start | bytes 524288 | tf_op jit(solution)/shard_map/all_to_all | solution.py:232
  522.3 48.7 %all-to-all-start.10 = ((f32[1,48,64,128]{3,2,0,1:T(8,128)}), f32[1,48,64,128]{3,2,0,1:T(8,128)}, u32[]{:S(2)}, u32[]{:S(2)}) async-start(f32[1,48,64,128]{3,2,0,1:T(8,128)} %convolution_bitcast_fusion), calls=%async_computation.10 | async-start | bytes 3145728 | tf_op jit(solution)/shard_map/all_to_all | solution.py:185
  535.5 40.6 %copy-start.20 = (f32[16,64,64]{2,1,0:T(8,128)S(1)}, f32[16,64,64]{2,1,0:T(8,128)}, u32[]{:S(2)}) copy-start(f32[16,64,64]{2,1,0:T(8,128)} %copy-done.19) | copy-start | bytes 786436
  571.0 45.8 %all-to-all-start.8 = ((f32[1,48,64,128]{3,2,0,1:T(8,128)}), f32[1,48,64,128]{3,2,0,1:T(8,128)S(1)}, u32[]{:S(2)}, u32[]{:S(2)}) async-start(f32[1,48,64,128]{3,2,0,1:T(8,128)} %multiply_bitcast_fusion), calls=%async_computation.8 | async-start | bytes 3145728 | tf_op jit(solution)/shard_map/all_to_all | solution.py:184
  578.9 46.6 %collective-permute-start.5 = (bf16[1,1,64,128]{3,2,1,0:T(8,128)(2,1)S(1)}, bf16[1,1,64,128]{3,2,1,0:T(8,128)(2,1)S(1)}, u32[]{:S(2)}, u32[]{:S(2)}) collective-permute-start(bf16[1,1,64,128]{3,2,1,0:T(8,128)(2,1)S(1)} %fusion.58), channel_id=1, source_target_pairs={{0,16},{16,32},{32,48},{48,64},{64,80},{80,96},{96,112},{112,128},... | collective-permute-start | bytes 49160 | tf_op jit(solution)/shard_map/ppermute | solution.py:21
  582.6 42.2 %collective-permute-start.4 = (bf16[1,1,64,128]{3,2,1,0:T(8,128)(2,1)S(1)}, bf16[1,1,64,128]{3,2,1,0:T(8,128)(2,1)}, u32[]{:S(2)}, u32[]{:S(2)}) collective-permute-start(bf16[1,1,64,128]{3,2,1,0:T(8,128)(2,1)S(1)} %fusion.59), channel_id=1, source_target_pairs={{16,0},{32,16},{48,32},{64,48},{80,64},{96,80},{112,96},{128,112},... | collective-permute-start | bytes 49160 | tf_op jit(solution)/shard_map/ppermute | solution.py:21
  588.0 21.5 %collective-permute-start.6 = (bf16[1,1,64,128]{3,2,1,0:T(8,128)(2,1)}, bf16[1,1,64,128]{3,2,1,0:T(8,128)(2,1)}, u32[]{:S(2)}, u32[]{:S(2)}) collective-permute-start(bf16[1,1,64,128]{3,2,1,0:T(8,128)(2,1)} %fusion.56), channel_id=1, source_target_pairs={{16,0},{32,16},{48,32},{64,48},{80,64},{96,80},{112,96},{128,112},... | collective-permute-start | bytes 49160 | tf_op jit(solution)/shard_map/ppermute | solution.py:21
  591.2 21.5 %collective-permute-start.7 = (bf16[1,1,64,128]{3,2,1,0:T(8,128)(2,1)}, bf16[1,1,64,128]{3,2,1,0:T(8,128)(2,1)}, u32[]{:S(2)}, u32[]{:S(2)}) collective-permute-start(bf16[1,1,64,128]{3,2,1,0:T(8,128)(2,1)} %fusion.57), channel_id=1, source_target_pairs={{0,16},{16,32},{32,48},{48,64},{64,80},{80,96},{96,112},{112,128},... | collective-permute-start | bytes 49160 | tf_op jit(solution)/shard_map/ppermute | solution.py:21
  616.8 16.1 %all-to-all-start.11 = ((bf16[16,2,4096]{2,1,0:T(2,128)(2,1)}), bf16[16,2,4096]{2,1,0:T(2,128)(2,1)S(1)}, u32[]{:S(2)}, u32[]{:S(2)}) async-start(bf16[16,2,4096]{2,1,0:T(2,128)(2,1)} %reshape.1104), calls=%async_computation.11 | async-start | bytes 524288 | tf_op jit(solution)/shard_map/all_to_all | solution.py:234
  632.9 17.5 %all-to-all-start.9 = ((bf16[16,2,4096]{2,1,0:T(2,128)(2,1)}), bf16[16,2,4096]{2,1,0:T(2,128)(2,1)S(1)}, u32[]{:S(2)}, u32[]{:S(2)}) async-start(bf16[16,2,4096]{2,1,0:T(2,128)(2,1)} %reshape.1102), calls=%async_computation.9 | async-start | bytes 524288 | tf_op jit(solution)/shard_map/all_to_all | solution.py:233
  (48 other events, 297.6 us)
Sparse Core Ops, SparseCore 0:
  167.2 148.3 all-reduce.16
  339.4 145.4 all-reduce.14
where the time goes:
time: 661 us; the launch traced here: 658 us
  waiting for transfers between devices  361 us (55%)
  starting transfers between devices  116 us (18%)
  local copies, waits for them, and re-layouts  67.5 us (10%)
  blocking collectives  36.8 us (6%)
  other arithmetic  33.5 us (5%)
  matrix products  28.9 us (4%)
  between operations  15.3 us (2%)
    psum x1, waiting for transfers between devices, per_device(): lax.psum(spread_q.astype(jnp.bfloat16), 'seq').astype(jnp.float32)  145 us
    psum x1, waiting for transfers between devices, spread(): return lax.psum(kept, axis)  108 us
    psum x1, blocking collectives, spread(): return lax.psum(kept, axis)  36.8 us
    all_to_all x1, waiting for transfers between devices, per_device(): lax.all_to_all(part_v, 'seq', split_axis=1, concat_axis=1, tiled=True)  35.5 us
    gather x48, local copies, waits for them, and re-layouts  32 us
    ppermute x8, starting transfers between devices, passed_along(): lax.ppermute(value, axis, [(source, source + steps) for source in range(i...  29.1 us
    all_to_all x1, starting transfers between devices, per_device(): lax.all_to_all(value_blk[:, send_ids], 'seq', split_axis=1, concat_axis=1...  14.9 us
    all_to_all x1, waiting for transfers between devices, per_device(): lax.all_to_all(to_heads(value), 'head', split_axis=0, concat_axis=1, tile...  13.9 us
  transfers between devices with their start and end apart: 22, of which 12 were waited for; matrix products, arithmetic and copies ran while one was open for 16% of the time, Pallas kernels for 0%

commit v1 on v0

--- a/solution.py
+++ b/solution.py
@@ -148,7 +148,7 @@
     totals_k, totals_v, totals_q = (
         lax.psum(key_part_k.astype(jnp.bfloat16), "seq").astype(jnp.float32),
         lax.psum(key_part_v.astype(jnp.bfloat16), "seq").astype(jnp.float32),
-        lax.psum(spread_q.astype(jnp.bfloat16), "seq").astype(jnp.float32),
+        jnp.sum(lax.all_gather(spread_q.astype(jnp.bfloat16), "seq"), axis=0).astype(jnp.float32),
     )
     grad_query = grad_query.at[:, :GLOB].add(at_home * totals_q.reshape(heads_here, GLOB, BLK, HD))
     grad_key_home = grad_key_home.at[:, :GLOB].add(

time: 661 us -> 700 us (1.059)
  blocking collectives: 36.8 us -> 81.2 us
    psum x1 -> x0, waiting for transfers between devices: 145 us -> none  [per_device(): lax.psum(spread_q.astype(jnp.bfloat16), 'seq').astype(jnp.float32)]
    psum x1 -> x2, waiting for transfers between devices: 108 us -> 251 us  [spread(): return lax.psum(kept, axis)]
    all_gather x0 -> x1, blocking collectives: none -> 43.2 us  [per_device(): lax.all_gather(spread_q.astype(jnp.bfloat16), 'seq')]
  transfers between devices with their start and end apart: 22 -> 22, of which waited for: 12 -> 12; matrix products, arithmetic and copies ran while one was open for 16% -> 15% of each run, Pallas kernels for 0% -> 0%
where the time goes in v1:
time: 700 us; the launch traced here: 698 us
  waiting for transfers between devices  360 us (51%)
  starting transfers between devices  112 us (16%)
  blocking collectives  81.2 us (12%)
  local copies, waits for them, and re-layouts  69.3 us (10%)
  other arithmetic  30.2 us (4%)
  matrix products  28.8 us (4%)
  between operations  15.4 us (2%)
    psum x2, waiting for transfers between devices, spread(): return lax.psum(kept, axis)  251 us
    all_gather x1, blocking collectives, per_device(): lax.all_gather(spread_q.astype(jnp.bfloat16), 'seq')  43.2 us
    psum x1, blocking collectives, spread(): return lax.psum(kept, axis)  38 us
    all_to_all x1, waiting for transfers between devices, per_device(): lax.all_to_all(part_v, 'seq', split_axis=1, concat_axis=1, tiled=True)  34.3 us
    gather x48, local copies, waits for them, and re-layouts  32 us
    ppermute x8, starting transfers between devices, passed_along(): lax.ppermute(value, axis, [(source, source + steps) for source in range(i...  29.1 us
    all_to_all x1, starting transfers between devices, per_device(): lax.all_to_all(value_blk[:, send_ids], 'seq', split_axis=1, concat_axis=1...  14.8 us
  transfers between devices with their start and end apart: 22, of which 12 were waited for; matrix products, arithmetic and copies ran while one was open for 15% of the time, Pallas kernels for 0%

profile of v1, /device:TPU:64, one launch (start us, length us, event | category | flops | bytes accessed | tf_op | source)
XLA Modules:
  0.0 697.5 jit_solution(8838742745156274583)
XLA Ops:
  8.9 9.2 %all-to-all-start = ((bf16[16,64,128]{2,1,0:T(8,128)(2,1)}), bf16[16,64,128]{2,1,0:T(8,128)(2,1)S(1)}, u32[]{:S(2)}, u32[]{:S(2)}) async-start(bf16[16,64,128]{2,1,0:T(8,128)(2,1)} %bitcast_bitcast_fusion.4), calls=%async_computation | async-start | bytes 524288 | tf_op jit(solution)/shard_map/all_to_all | solution.py:82
  18.2 32.0 %while.10 = (s32[]{:T(128)}, s32[256,3]{0,1:T(4,128)}, s32[16,2]{0,1:T(2,128)S(1)}, s32[16,16,3]{1,2,0:T(4,128)S(1)}, s32[]{:T(128)}) while((s32[]{:T(128)}, s32[256,3]{0,1:T(4,128)}, s32[16,2]{0,1:T(2,128)S(1)}, s32[16,16,3]{1,2,0:T(4,128)S(1)}, s32[]{:T(128)}) %tuple.65), condition=%wide.while_cond.9, body=%wide.while_body.9.sunk | while | flops 2 | bytes 2345 | solution.py:58
  51.5 5.3 gather_fusion.6
  61.5 9.6 %all-to-all-start.2 = ((bf16[16,64,128]{2,1,0:T(8,128)(2,1)}), bf16[16,64,128]{2,1,0:T(8,128)(2,1)S(1)}, u32[]{:S(2)}, u32[]{:S(2)}) async-start(bf16[16,64,128]{2,1,0:T(8,128)(2,1)} %bitcast_bitcast_fusion.2), calls=%async_computation.2 | async-start | bytes 524288 | tf_op jit(solution)/shard_map/all_to_all | solution.py:83
  72.6 13.3 %all-to-all-done.2 = bf16[16,64,128]{2,1,0:T(8,128)(2,1)S(1)} async-done(((bf16[16,64,128]{2,1,0:T(8,128)(2,1)}), bf16[16,64,128]{2,1,0:T(8,128)(2,1)S(1)}, u32[]{:S(2)}, u32[]{:S(2)}) %all-to-all-start.2) | async-done | bytes 262176 | tf_op jit(solution)/shard_map/all_to_all | solution.py:83
  85.9 3.5 all-to-all-start.4
  91.1 11.3 %all-to-all-done.4 = bf16[16,64,128]{2,1,0:T(8,128)(2,1)S(1)} async-done(((bf16[16,64,128]{2,1,0:T(8,128)(2,1)}), bf16[16,64,128]{2,1,0:T(8,128)(2,1)S(1)}, u32[]{:S(2)}, u32[]{:S(2)}) %all-to-all-start.4) | async-done | bytes 262176 | tf_op jit(solution)/shard_map/all_to_all | solution.py:84
  102.4 3.5 all-to-all-start.3
  109.7 8.2 %all-to-all-done.3 = bf16[16,64,128]{2,1,0:T(8,128)(2,1)S(1)} async-done(((bf16[16,64,128]{2,1,0:T(8,128)(2,1)}), bf16[16,64,128]{2,1,0:T(8,128)(2,1)S(1)}, u32[]{:S(2)}, u32[]{:S(2)}) %all-to-all-start.3) | async-done | bytes 262176 | tf_op jit(solution)/shard_map/all_to_all | solution.py:85
  118.0 3.5 all-to-all-start.1
  123.3 10.1 %all-to-all-done.1 = bf16[16,64,128]{2,1,0:T(8,128)(2,1)S(1)} async-done(((bf16[16,64,128]{2,1,0:T(8,128)(2,1)}), bf16[16,64,128]{2,1,0:T(8,128)(2,1)S(1)}, u32[]{:S(2)}, u32[]{:S(2)}) %all-to-all-start.1) | async-done | bytes 262176 | tf_op jit(solution)/shard_map/all_to_all | solution.py:81
  134.7 5.4 collective-permute-start.2
  142.6 6.0 collective-permute-start.3
  155.6 7.3 %all-to-all-start.5 = ((bf16[1,48,64,128]{3,2,0,1:T(8,128)(2,1)}), bf16[1,48,64,128]{3,2,0,1:T(8,128)(2,1)}, u32[]{:S(2)}, u32[]{:S(2)}) async-start(bf16[1,48,64,128]{3,2,0,1:T(8,128)(2,1)} %bitcast.32), calls=%async_computation.5 | async-start | bytes 1572864 | tf_op jit(solution)/shard_map/all_to_all | solution.py:168
  169.3 38.0 %all-reduce.9 = (f32[128]{0:T(128)}, f32[128]{0:T(128)}) all-reduce(f32[128]{0:T(128)S(1)} %fusion.112, f32[128]{0:T(128)S(1)} %copy-done.48), channel_id=1, replica_groups=mesh['seq'=16,'head'=16] {'seq'}, use_global_device_ids=true, to_apply=%region_4.5 | all-reduce | flops 256 | bytes 2048 | tf_op jit(solution)/shard_map/psum | solution.py:15
  209.1 97.4 %all-reduce.17.cloned.1.call-done = (bf16[128,128]{1,0:T(8,128)(2,1)}, bf16[128,128]{1,0:T(8,128)(2,1)}) async-done(((bf16[128,128]{1,0:T(8,128)(2,1)}, bf16[128,128]{1,0:T(8,128)(2,1)}), (bf16[128,128]{1,0:T(8,128)(2,1)}, bf16[128,128]{1,0:T(8,128)(2,1)})) %all-reduce.17.cloned.1.call-update) | async-done | bytes 65552 | tf_op jit(solution)/shard_map/psum | solution.py:15
  311.9 153.1 %all-reduce.15.cloned.1.call-done = (bf16[128,128]{1,0:T(8,128)(2,1)}, bf16[128,128]{1,0:T(8,128)(2,1)}, bf16[1,128,128]{2,1,0:T(8,128)(2,1)}, bf16[1,128,128]{2,1,0:T(8,128)(2,1)}) async-done(((bf16[128,128]{1,0:T(8,128)(2,1)}, bf16[128,128]{1,0:T(8,128)(2,1)}, bf16[1,128,128]{2,1,0:T(8,128)(2,1)}, bf16[1,128,128]{2,1,0:T(8,128)(2,1)}), (bf16[128,128]{1,0:T(8,128)(2,1)}, bf16[128,128]{1,0:T(8,128)(2,1)}, ...) | async-done | bytes 131088 | tf_op jit(solution)/shard_map/psum | solution.py:15
  466.0 14.8 %all-to-all-start.6 = ((bf16[1,48,64,128]{3,2,0,1:T(8,128)(2,1)}), bf16[1,48,64,128]{3,2,0,1:T(8,128)(2,1)}, u32[]{:S(2)}, u32[]{:S(2)}) async-start(bf16[1,48,64,128]{3,2,0,1:T(8,128)(2,1)} %bitcast.348), calls=%async_computation.6 | async-start | bytes 1572864 | tf_op jit(solution)/shard_map/all_to_all | solution.py:169
  481.3 43.2 %all-gather = bf16[2048,128]{1,0:T(8,128)(2,1)} all-gather(bf16[128,128]{1,0:T(8,128)(2,1)S(1)} %fusion.35), channel_id=2, replica_groups=mesh['seq'=16,'head'=16] {'seq'}, dimensions={0}, use_global_device_ids=true | all-gather | bytes 557056 | tf_op jit(solution)/shard_map/all_gather | solution.py:151
  533.7 5.4 scatter_fusion
  543.3 6.8 all-to-all-start.7
  553.1 9.1 %all-to-all-done.7 = bf16[16,2,4096]{2,1,0:T(2,128)(2,1)S(1)} async-done(((bf16[16,2,4096]{2,1,0:T(2,128)(2,1)}), bf16[16,2,4096]{2,1,0:T(2,128)(2,1)S(1)}, u32[]{:S(2)}, u32[]{:S(2)}) %all-to-all-start.7) | async-done | bytes 262176 | tf_op jit(solution)/shard_map/all_to_all | solution.py:232
  562.9 8.3 %all-to-all-start.10 = ((f32[1,48,64,128]{3,2,0,1:T(8,128)}), f32[1,48,64,128]{3,2,0,1:T(8,128)S(1)}, u32[]{:S(2)}, u32[]{:S(2)}) async-start(f32[1,48,64,128]{3,2,0,1:T(8,128)} %convolution_bitcast_fusion), calls=%async_computation.10 | async-start | bytes 3145728 | tf_op jit(solution)/shard_map/all_to_all | solution.py:185
  573.9 34.3 %all-to-all-done.10 = f32[1,48,64,128]{3,2,0,1:T(8,128)S(1)} async-done(((f32[1,48,64,128]{3,2,0,1:T(8,128)}), f32[1,48,64,128]{3,2,0,1:T(8,128)S(1)}, u32[]{:S(2)}, u32[]{:S(2)}) %all-to-all-start.10) | async-done | bytes 1572896 | tf_op jit(solution)/shard_map/all_to_all | solution.py:185
  609.3 5.1 all-to-all-start.8
  621.5 4.6 collective-permute-start.4
  637.2 5.4 scatter_fusion.2
  642.6 5.2 collective-permute-done.6
  654.4 6.4 all-to-all-start.11
  668.0 4.7 all-to-all-done.11
  672.7 5.0 all-to-all-start.9
  679.8 9.8 %all-to-all-done.9 = bf16[16,2,4096]{2,1,0:T(2,128)(2,1)S(1)} async-done(((bf16[16,2,4096]{2,1,0:T(2,128)(2,1)}), bf16[16,2,4096]{2,1,0:T(2,128)(2,1)S(1)}, u32[]{:S(2)}, u32[]{:S(2)}) %all-to-all-start.9) | async-done | bytes 262176 | tf_op jit(solution)/shard_map/all_to_all | solution.py:233
  (313 shorter events, 129.3 us)
Async XLA Ops:
  8.9 52.7 %all-to-all-start = ((bf16[16,64,128]{2,1,0:T(8,128)(2,1)}), bf16[16,64,128]{2,1,0:T(8,128)(2,1)S(1)}, u32[]{:S(2)}, u32[]{:S(2)}) async-start(bf16[16,64,128]{2,1,0:T(8,128)(2,1)} %bitcast_bitcast_fusion.4), calls=%async_computation | async-start | bytes 524288 | tf_op jit(solution)/shard_map/all_to_all | solution.py:82
  61.5 24.4 %all-to-all-start.2 = ((bf16[16,64,128]{2,1,0:T(8,128)(2,1)}), bf16[16,64,128]{2,1,0:T(8,128)(2,1)S(1)}, u32[]{:S(2)}, u32[]{:S(2)}) async-start(bf16[16,64,128]{2,1,0:T(8,128)(2,1)} %bitcast_bitcast_fusion.2), calls=%async_computation.2 | async-start | bytes 524288 | tf_op jit(solution)/shard_map/all_to_all | solution.py:83
  85.9 16.4 %all-to-all-start.4 = ((bf16[16,64,128]{2,1,0:T(8,128)(2,1)}), bf16[16,64,128]{2,1,0:T(8,128)(2,1)S(1)}, u32[]{:S(2)}, u32[]{:S(2)}) async-start(bf16[16,64,128]{2,1,0:T(8,128)(2,1)} %bitcast_bitcast_fusion), calls=%async_computation.4 | async-start | bytes 524288 | tf_op jit(solution)/shard_map/all_to_all | solution.py:84
  102.4 15.6 %all-to-all-start.3 = ((bf16[16,64,128]{2,1,0:T(8,128)(2,1)}), bf16[16,64,128]{2,1,0:T(8,128)(2,1)S(1)}, u32[]{:S(2)}, u32[]{:S(2)}) async-start(bf16[16,64,128]{2,1,0:T(8,128)(2,1)} %bitcast_bitcast_fusion.1), calls=%async_computation.3 | async-start | bytes 524288 | tf_op jit(solution)/shard_map/all_to_all | solution.py:85
  118.0 15.5 %all-to-all-start.1 = ((bf16[16,64,128]{2,1,0:T(8,128)(2,1)}), bf16[16,64,128]{2,1,0:T(8,128)(2,1)S(1)}, u32[]{:S(2)}, u32[]{:S(2)}) async-start(bf16[16,64,128]{2,1,0:T(8,128)(2,1)} %bitcast_bitcast_fusion.3), calls=%async_computation.1 | async-start | bytes 524288 | tf_op jit(solution)/shard_map/all_to_all | solution.py:81
  123.3 41.0 %copy-start.23 = (bf16[1,15,64,128]{3,2,1,0:T(8,128)(2,1)}, bf16[1,15,64,128]{3,2,1,0:T(8,128)(2,1)S(1)}, u32[]{:S(2)}) copy-start(bf16[1,15,64,128]{3,2,1,0:T(8,128)(2,1)S(1)} %get-tuple-element.147) | copy-start | bytes 737284
  134.7 72.6 %collective-permute-start.2 = (bf16[1,1,64,128]{3,2,1,0:T(8,128)(2,1)S(1)}, bf16[1,1,64,128]{3,2,1,0:T(8,128)(2,1)S(1)}, u32[]{:S(2)}, u32[]{:S(2)}) collective-permute-start(bf16[1,1,64,128]{3,2,1,0:T(8,128)(2,1)S(1)} %get-tuple-element.143), channel_id=1, source_target_pairs={{16,0},{32,16},{48,32},{64,48},{80,64},{96,80},{112,96},{128,112},... | collective-permute-start | bytes 49160 | tf_op jit(solution)/shard_map/ppermute | solution.py:21
  140.1 67.4 %collective-permute-start = (bf16[1,1,64,128]{3,2,1,0:T(8,128)(2,1)S(1)}, bf16[1,1,64,128]{3,2,1,0:T(8,128)(2,1)S(1)}, u32[]{:S(2)}, u32[]{:S(2)}) collective-permute-start(bf16[1,1,64,128]{3,2,1,0:T(8,128)(2,1)S(1)} %get-tuple-element.144), channel_id=1, source_target_pairs={{0,16},{16,32},{32,48},{48,64},{64,80},{80,96},{96,112},{112,128},... | collective-permute-start | bytes 49160 | tf_op jit(solution)/shard_map/ppermute | solution.py:21
  142.6 64.8 %collective-permute-start.3 = (bf16[1,1,64,128]{3,2,1,0:T(8,128)(2,1)S(1)}, bf16[1,1,64,128]{3,2,1,0:T(8,128)(2,1)S(1)}, u32[]{:S(2)}, u32[]{:S(2)}) collective-permute-start(bf16[1,1,64,128]{3,2,1,0:T(8,128)(2,1)S(1)} %get-tuple-element.141), channel_id=1, source_target_pairs={{16,0},{32,16},{48,32},{64,48},{80,64},{96,80},{112,96},{128,112},... | collective-permute-start | bytes 49160 | tf_op jit(solution)/shard_map/ppermute | solution.py:21
  148.6 60.4 %collective-permute-start.1 = (bf16[1,1,64,128]{3,2,1,0:T(8,128)(2,1)}, bf16[1,1,64,128]{3,2,1,0:T(8,128)(2,1)S(1)}, u32[]{:S(2)}, u32[]{:S(2)}) collective-permute-start(bf16[1,1,64,128]{3,2,1,0:T(8,128)(2,1)} %get-tuple-element.142), channel_id=1, source_target_pairs={{0,16},{16,32},{32,48},{48,64},{64,80},{80,96},{96,112},{112,128},... | collective-permute-start | bytes 49160 | tf_op jit(solution)/shard_map/ppermute | solution.py:21
  155.6 310.4 %all-to-all-start.5 = ((bf16[1,48,64,128]{3,2,0,1:T(8,128)(2,1)}), bf16[1,48,64,128]{3,2,0,1:T(8,128)(2,1)}, u32[]{:S(2)}, u32[]{:S(2)}) async-start(bf16[1,48,64,128]{3,2,0,1:T(8,128)(2,1)} %bitcast.32), calls=%async_computation.5 | async-start | bytes 1572864 | tf_op jit(solution)/shard_map/all_to_all | solution.py:168
  163.0 143.6 %all-reduce.17.cloned.1.call-start = ((), (), s32[]{:S(2)}) async-start(), calls=%async_computation.13 | async-start | bytes 131072 | tf_op jit(solution)/shard_map/psum | solution.py:15
  163.7 301.3 %all-reduce.15.cloned.1.call-start = ((), (), s32[]{:S(2)}) async-start(), calls=%async_computation.12 | async-start | bytes 262144 | tf_op jit(solution)/shard_map/psum | solution.py:15
  164.9 145.7 %copy-start.11 = (bf16[16,64,64]{2,1,0:T(8,128)(2,1)}, bf16[16,64,64]{2,1,0:T(8,128)(2,1)S(1)}, u32[]{:S(2)}) copy-start(bf16[16,64,64]{2,1,0:T(8,128)(2,1)S(1)} %fusion.34) | copy-start | bytes 393220
  167.0 40.3 %copy-start.47 = (f32[64]{0:T(128)S(1)}, f32[64]{0:T(128)}, u32[]{:S(2)}) copy-start(f32[64]{0:T(128)} %get-tuple-element.151) | copy-start | bytes 772
  167.0 41.2 %copy-start.46 = (f32[64]{0:T(128)S(1)}, f32[64]{0:T(128)}, u32[]{:S(2)}) copy-start(f32[64]{0:T(128)} %get-tuple-element.152) | copy-start | bytes 772
  167.0 139.6 %copy-start.41 = (pred[1024]{0:T(1024)(128)(4,1)S(1)}, pred[1024]{0:T(1024)(128)(4,1)}, u32[]{:S(2)}) copy-start(pred[1024]{0:T(1024)(128)(4,1)} %broadcast_in_dim.110) | copy-start | bytes 3076
  311.8 169.0 %copy-start.44 = (f32[128]{0:T(128)S(1)}, f32[128]{0:T(128)}, u32[]{:S(2)}) copy-start(f32[128]{0:T(128)} %get-tuple-element.132) | copy-start | bytes 1540
  466.0 62.8 %all-to-all-start.6 = ((bf16[1,48,64,128]{3,2,0,1:T(8,128)(2,1)}), bf16[1,48,64,128]{3,2,0,1:T(8,128)(2,1)}, u32[]{:S(2)}, u32[]{:S(2)}) async-start(bf16[1,48,64,128]{3,2,0,1:T(8,128)(2,1)} %bitcast.348), calls=%async_computation.6 | async-start | bytes 1572864 | tf_op jit(solution)/shard_map/all_to_all | solution.py:169
  480.8 44.9 %copy-start.36 = (f32[48,64]{1,0:T(8,128)S(1)}, f32[48,64]{1,0:T(8,128)}, u32[]{:S(2)}) copy-start(f32[48,64]{1,0:T(8,128)} %gather_fusion.2) | copy-start | bytes 36868
  480.8 44.9 %copy-start.45 = (pred[48]{0:T(512)(128)(4,1)S(1)}, pred[48]{0:T(512)(128)(4,1)}, u32[]{:S(2)}) copy-start(pred[48]{0:T(512)(128)(4,1)} %get-tuple-element.139) | copy-start | bytes 148
  481.1 43.4 %copy-start.7 = (bf16[128,1024]{1,0:T(8,128)(2,1)}, bf16[128,1024]{1,0:T(8,128)(2,1)S(1)}, u32[]{:S(2)}) copy-start(bf16[128,1024]{1,0:T(8,128)(2,1)S(1)} %fusion.30) | copy-start | bytes 786436
  543.3 18.9 %all-to-all-start.7 = ((bf16[16,2,4096]{2,1,0:T(2,128)(2,1)}), bf16[16,2,4096]{2,1,0:T(2,128)(2,1)S(1)}, u32[]{:S(2)}, u32[]{:S(2)}) async-start(bf16[16,2,4096]{2,1,0:T(2,128)(2,1)} %reshape.1110), calls=%async_computation.7 | async-start | bytes 524288 | tf_op jit(solution)/shard_map/all_to_all | solution.py:232
  562.9 45.3 %all-to-all-start.10 = ((f32[1,48,64,128]{3,2,0,1:T(8,128)}), f32[1,48,64,128]{3,2,0,1:T(8,128)S(1)}, u32[]{:S(2)}, u32[]{:S(2)}) async-start(f32[1,48,64,128]{3,2,0,1:T(8,128)} %convolution_bitcast_fusion), calls=%async_computation.10 | async-start | bytes 3145728 | tf_op jit(solution)/shard_map/all_to_all | solution.py:185
  573.9 40.5 %copy-start.16 = (f32[16,64,64]{2,1,0:T(8,128)S(1)}, f32[16,64,64]{2,1,0:T(8,128)}, u32[]{:S(2)}) copy-start(f32[16,64,64]{2,1,0:T(8,128)} %copy-done.15) | copy-start | bytes 786436
  609.3 45.1 %all-to-all-start.8 = ((f32[1,48,64,128]{3,2,0,1:T(8,128)}), f32[1,48,64,128]{3,2,0,1:T(8,128)S(1)}, u32[]{:S(2)}, u32[]{:S(2)}) async-start(f32[1,48,64,128]{3,2,0,1:T(8,128)} %multiply_bitcast_fusion), calls=%async_computation.8 | async-start | bytes 3145728 | tf_op jit(solution)/shard_map/all_to_all | solution.py:184
  617.2 47.4 %collective-permute-start.5 = (bf16[1,1,64,128]{3,2,1,0:T(8,128)(2,1)S(1)}, bf16[1,1,64,128]{3,2,1,0:T(8,128)(2,1)S(1)}, u32[]{:S(2)}, u32[]{:S(2)}) collective-permute-start(bf16[1,1,64,128]{3,2,1,0:T(8,128)(2,1)S(1)} %fusion.57), channel_id=1, source_target_pairs={{0,16},{16,32},{32,48},{48,64},{64,80},{80,96},{96,112},{112,128},... | collective-permute-start | bytes 49160 | tf_op jit(solution)/shard_map/ppermute | solution.py:21
  621.5 43.1 %collective-permute-start.4 = (bf16[1,1,64,128]{3,2,1,0:T(8,128)(2,1)}, bf16[1,1,64,128]{3,2,1,0:T(8,128)(2,1)S(1)}, u32[]{:S(2)}, u32[]{:S(2)}) collective-permute-start(bf16[1,1,64,128]{3,2,1,0:T(8,128)(2,1)} %fusion.58), channel_id=1, source_target_pairs={{16,0},{32,16},{48,32},{64,48},{80,64},{96,80},{112,96},{128,112},... | collective-permute-start | bytes 49160 | tf_op jit(solution)/shard_map/ppermute | solution.py:21
  626.8 21.0 %collective-permute-start.6 = (bf16[1,1,64,128]{3,2,1,0:T(8,128)(2,1)}, bf16[1,1,64,128]{3,2,1,0:T(8,128)(2,1)S(1)}, u32[]{:S(2)}, u32[]{:S(2)}) collective-permute-start(bf16[1,1,64,128]{3,2,1,0:T(8,128)(2,1)} %fusion.55), channel_id=1, source_target_pairs={{16,0},{32,16},{48,32},{64,48},{80,64},{96,80},{112,96},{128,112},... | collective-permute-start | bytes 49160 | tf_op jit(solution)/shard_map/ppermute | solution.py:21
  629.5 21.5 %collective-permute-start.7 = (bf16[1,1,64,128]{3,2,1,0:T(8,128)(2,1)S(1)}, bf16[1,1,64,128]{3,2,1,0:T(8,128)(2,1)S(1)}, u32[]{:S(2)}, u32[]{:S(2)}) collective-permute-start(bf16[1,1,64,128]{3,2,1,0:T(8,128)(2,1)S(1)} %fusion.56), channel_id=1, source_target_pairs={{0,16},{16,32},{32,48},{48,64},{64,80},{80,96},{96,112},{112,128},... | collective-permute-start | bytes 49160 | tf_op jit(solution)/shard_map/ppermute | solution.py:21
  654.4 18.3 %all-to-all-start.11 = ((bf16[16,2,4096]{2,1,0:T(2,128)(2,1)}), bf16[16,2,4096]{2,1,0:T(2,128)(2,1)S(1)}, u32[]{:S(2)}, u32[]{:S(2)}) async-start(bf16[16,2,4096]{2,1,0:T(2,128)(2,1)} %reshape.1114), calls=%async_computation.11 | async-start | bytes 524288 | tf_op jit(solution)/shard_map/all_to_all | solution.py:234
  672.7 16.9 %all-to-all-start.9 = ((bf16[16,2,4096]{2,1,0:T(2,128)(2,1)}), bf16[16,2,4096]{2,1,0:T(2,128)(2,1)S(1)}, u32[]{:S(2)}, u32[]{:S(2)}) async-start(bf16[16,2,4096]{2,1,0:T(2,128)(2,1)} %reshape.1112), calls=%async_computation.9 | async-start | bytes 524288 | tf_op jit(solution)/shard_map/all_to_all | solution.py:233
  (41 other events, 260.9 us)
Sparse Core Ops, SparseCore 0:
  167.1 139.4 all-reduce.16
  310.4 154.4 all-reduce.14
